TPU v7x, 256 devices: a whole 4x4x8 slice. The times are simulated.
256 devices in a mesh: seq: 32 (over z_hi, x, core), head: 8 (over y, z_lo).
Axes of the slice: x: 4, y: 4, z: 8 (z_hi: 4, z_lo: 2; z = z_hi * 2 + z_lo), core: 2. Of those that a mesh axis runs over, the one named last changes fastest.
Arguments:
- queries: bfloat16 [6144, 4096], P('seq', 'head'), may hold values from -12.5 to 12.5
- keys: bfloat16 [6144, 1024], P('seq', 'head'), may hold values from -10.5 to 10.5
- values: bfloat16 [6144, 1024], P('seq', 'head'), may hold values from -6 to 6
- d_out: bfloat16 [6144, 4096], P('seq', 'head'), may hold values from -6 to 6
- w_out: bfloat16 [4096, 4096], P('head'), may hold values from -0.09375 to 0.09375
- doc_starts: int32 [4], replicated, may hold values from 0 to 6128, as said below
Outputs:
- query_grad: bfloat16 [6144, 4096], P('seq', 'head')
- key_grad: bfloat16 [6144, 1024], P('seq', 'head')
- value_grad: bfloat16 [6144, 1024], P('seq', 'head')
Inputs may be any that keep to these rules, and one draw needn't show every extreme that they name: doc_starts[0] is 0, the entries rise strictly, every entry is a multiple of 16, and the last entry is 6128, so the last document has 16 positions; a document runs from its start to the next start or to the end of the sequence.
All inputs are finite; a program needn't handle non-finite values.
Results may differ from a plain program's by a relative error of at most 0.0163.
Values may be sent and summed in bfloat16 or wider, within the bound.
A program may use at most 128 MiB of HBM per device.

v0:
```python
import math
import jax
import jax.numpy as jnp
from jax import lax
from jax.sharding import PartitionSpec as P

DH = 128
NEG_FILL = -1e30


def doc_index(doc_starts, places):
    return jnp.sum((places[:, None] >= doc_starts[None, :]).astype(jnp.int32), axis=1)


def allowed_pairs(doc_starts, row_ids, col_ids):
    earlier = col_ids[None, :] <= row_ids[:, None]
    same_doc = doc_index(doc_starts, row_ids)[:, None] == doc_index(doc_starts, col_ids)[None, :]
    return (earlier & same_doc)[None, None]


def softmax_grads(q_four, g_four, key_three, value_three, allowed, log_total, row_delta, scaling):
    scores = (
        jnp.einsum("sghd,kgd->ghsk", q_four, key_three, preferred_element_type=jnp.float32)
        * scaling
    )
    prob_full = jnp.where(allowed, jnp.exp(scores - log_total[..., None]), 0.0)
    grad_dots = jnp.einsum(
        "sghd,kgd->ghsk", g_four, value_three, preferred_element_type=jnp.float32
    )
    dscores = prob_full * (grad_dots - row_delta[..., None]) * scaling
    return (prob_full.astype(jnp.bfloat16), dscores.astype(jnp.bfloat16))


def shards(queries, keys, values, d_out, w_out, doc_starts):
    rows_here = queries.shape[0]
    head_size = DH
    groups = keys.shape[1] // head_size
    per_group = queries.shape[1] // keys.shape[1]
    scaling = 1.0 / math.sqrt(head_size)
    first_row = lax.axis_index("seq") * rows_here
    my_rows = first_row + jnp.arange(rows_here, dtype=jnp.int32)
    weights = w_out
    attn_grad = lax.dot_general(
        lax.all_gather(d_out, "head", axis=1, tiled=True),
        weights,
        (((1,), (1,)), ((), ())),
        preferred_element_type=jnp.float32,
    )
    attn_grad = attn_grad.astype(jnp.bfloat16)
    query_four = queries.reshape(rows_here, groups, per_group, head_size)
    grad_four = attn_grad.reshape(rows_here, groups, per_group, head_size)
    stat_shape = (groups, per_group, rows_here)
    key_block = lax.all_gather(keys, "seq", axis=0, tiled=True)
    value_block = lax.all_gather(values, "seq", axis=0, tiled=True)
    piece_rows = key_block.shape[0]
    allowed = allowed_pairs(doc_starts, my_rows, jnp.arange(piece_rows, dtype=jnp.int32))
    key_three = key_block.reshape(piece_rows, groups, head_size)
    value_three = value_block.reshape(piece_rows, groups, head_size)
    scores = (
        jnp.einsum("sghd,kgd->ghsk", query_four, key_three, preferred_element_type=jnp.float32)
        * scaling
    )
    scores = jnp.where(allowed, scores, NEG_FILL)
    high_old = jnp.full(stat_shape, NEG_FILL, jnp.float32)
    high_new = jnp.maximum(high_old, jnp.max(scores, axis=-1))
    weights = jnp.where(allowed, jnp.exp(scores - high_new[..., None]), 0.0)
    grad_dots = jnp.einsum(
        "sghd,kgd->ghsk", grad_four, value_three, preferred_element_type=jnp.float32
    )
    total_new = jnp.sum(weights, axis=-1)
    accum_new = jnp.sum(weights * grad_dots, axis=-1)
    log_total = high_new + jnp.log(total_new)
    row_delta = accum_new / total_new
    key_block = lax.all_gather(keys, "seq", axis=0, tiled=True)
    value_block = lax.all_gather(values, "seq", axis=0, tiled=True)
    piece_rows = key_block.shape[0]
    allowed = allowed_pairs(doc_starts, my_rows, jnp.arange(piece_rows, dtype=jnp.int32))
    key_three = key_block.reshape(piece_rows, groups, head_size)
    value_three = value_block.reshape(piece_rows, groups, head_size)
    prob_half, dscores = softmax_grads(
        query_four, grad_four, key_three, value_three, allowed, log_total, row_delta, scaling
    )
    key_three, prob_half, dscores, piece_rows = (key_three, prob_half, dscores, piece_rows)
    query_acc = jnp.einsum("ghsk,kgd->sghd", dscores, key_three, preferred_element_type=jnp.float32)
    key_piece = jnp.einsum(
        "ghsk,sghd->kgd", dscores, query_four, preferred_element_type=jnp.float32
    )
    value_piece = jnp.einsum(
        "ghsk,sghd->kgd", prob_half, grad_four, preferred_element_type=jnp.float32
    )
    key_acc = key_piece
    value_acc = value_piece
    query_acc, key_terms, value_terms = (query_acc, key_acc, value_acc)
    key_acc, value_acc = (
        lax.psum_scatter(
            key_terms.astype(jnp.bfloat16), "seq", scatter_dimension=0, tiled=True
        ).astype(jnp.float32),
        lax.psum_scatter(
            value_terms.astype(jnp.bfloat16), "seq", scatter_dimension=0, tiled=True
        ).astype(jnp.float32),
    )
    query_grad = query_acc.reshape(rows_here, groups * per_group * head_size).astype(jnp.bfloat16)
    key_grad = key_acc.reshape(rows_here, groups * head_size).astype(jnp.bfloat16)
    value_grad = value_acc.reshape(rows_here, groups * head_size).astype(jnp.bfloat16)
    return (query_grad, key_grad, value_grad)


def solution(mesh):
    return jax.shard_map(
        shards,
        mesh=mesh,
        in_specs=(
            P("seq", "head"),
            P("seq", "head"),
            P("seq", "head"),
            P("seq", "head"),
            P("head", None),
            P(),
        ),
        out_specs=(P("seq", "head"), P("seq", "head"), P("seq", "head")),
        check_vma=False,
    )
```

profile of v0, /device:TPU:8, one launch (start us, length us, event | category | flops | bytes accessed | tf_op | source)
XLA Modules:
  0.0 378.5 jit_solution(6322208966597983329)
XLA Ops:
  7.2 0.0 copy-start
  7.2 0.0 all-gather.6.cloned.1.call-start
  7.2 0.7 all-gather.6.cloned.1.call-update
  7.9 0.0 all-gather.4.cloned.1.call-start
  8.0 0.7 all-gather.4.cloned.1.call-update
  8.7 0.0 all-gather.8.cloned.1.call-start
  8.7 0.7 all-gather.8.cloned.1.call-update
  9.4 0.0 reduce-scatter.7.cloned.1.call-start
  9.5 0.7 convert_reduce_fusion.1
  10.2 0.8 convert_reduce_fusion
  11.0 1.0 fusion.25
  12.0 45.0 %all-gather.6.cloned.1.call-done = bf16[192,4096]{1,0:T(8,128)(2,1)} async-done(((bf16[192,512]{1,0:T(8,128)(2,1)}), bf16[192,4096]{1,0:T(8,128)(2,1)}) %all-gather.6.cloned.1.call-update) | async-done | bytes 1572880 | tf_op jit(solution)/shard_map/all_gather | solution.py:44
  57.0 4.2 %fusion.38 = bf16[24,4,8,128]{3,2,1,0:T(8,128)(2,1)S(1)} fusion(bf16[192,4096]{1,0:T(8,128)(2,1)} %all-gather.6.cloned.1.call-done, bf16[512,4096]{1,0:T(8,128)(2,1)} %param.10), kind=kOutput, calls=%fused_computation.35 | convolution fusion | flops 805404672 | bytes 5963776 | tf_op jit(solution)/shard_map/dot_general | solution.py:43
  61.2 52.1 %all-gather.4.cloned.1.call-done = bf16[6144,128]{1,0:T(8,128)(2,1)} async-done(((bf16[192,128]{1,0:T(8,128)(2,1)}), bf16[6144,128]{1,0:T(8,128)(2,1)}) %all-gather.4.cloned.1.call-update) | async-done | bytes 1572880 | tf_op jit(solution)/shard_map/all_gather | solution.py:74
  113.3 0.0 copy-done
  113.3 9.9 %fusion.6 = (f32[4,192]{1,0:T(4,128)S(1)}, f32[6144,192,4]{0,1,2:T(8,128)}) fusion(pred[192,6144]{1,0:T(8,128)(4,1)S(1)} %fusion.25, bf16[6144,128]{1,0:T(8,128)(2,1)} %all-gather.4.cloned.1.call-done, bf16[192,512]{1,0:T(8,128)(2,1)S(1)} %copy-done), kind=kOutput, calls=%fused_computation.11 | convolution fusion | flops 1222114560 | bytes 21826560 | tf_op jit(solution)/shard_map/sghd,kgd->ghsk/dot_general | solution.py:23
  123.2 43.0 %all-gather.8.cloned.1.call-done = bf16[6144,128]{1,0:T(8,128)(2,1)} async-done(((bf16[192,128]{1,0:T(8,128)(2,1)}), bf16[6144,128]{1,0:T(8,128)(2,1)}) %all-gather.8.cloned.1.call-update) | async-done | bytes 1572880 | tf_op jit(solution)/shard_map/all_gather | solution.py:75
  166.2 15.5 %fusion.8 = (f32[4,192]{1,0:T(4,128)S(1)}, f32[4,192]{1,0:T(4,128)S(1)}, f32[192,4,6144]{2,0,1:T(8,128)}) fusion(f32[6144,192,4]{0,1,2:T(8,128)} %get-tuple-element.20, f32[4,192]{1,0:T(4,128)S(1)} %broadcast_maximum_fusion, pred[192,6144]{1,0:T(8,128)(4,1)S(1)} %fusion.25, bf16[6144,128]{1,0:T(8,128)(2,1)} %all-gather.8.cloned.1.call-done, ...), kind=kOutput, calls=%fused_computation.13 | convolution fusion | flops 1240988160 | bytes 40707072 | tf_op jit(solution)/shard_map/sghd,kgd->ghsk/dot_general | solution.py:27
  181.8 9.1 %fusion.21 = bf16[6144,128]{0,1:T(8,128)(2,1)S(1)} fusion(f32[6144,192,4]{0,1,2:T(8,128)} %get-tuple-element.20, f32[4,192]{1,0:T(4,128)S(1)} %get-tuple-element.17, pred[192,6144]{1,0:T(8,128)(4,1)S(1)} %fusion.25, bf16[24,4,8,128]{3,2,1,0:T(8,128)(2,1)S(1)} %fusion.38), kind=kOutput, calls=%fused_computation.22 | convolution fusion | flops 1227620352 | bytes 21826560 | tf_op jit(solution)/shard_map/ghsk,sghd->kgd/dot_general | solution.py:88
  190.8 1.6 copy.34
  192.4 0.0 reduce-scatter.7.cloned.1.call-update
  192.5 0.2 reduce-scatter.5.cloned.1.call-start
  192.7 13.7 %fusion.10 = bf16[4,192,6144]{2,1,0:T(8,128)(2,1)S(1)} fusion(f32[192,4,6144]{2,0,1:T(8,128)} %get-tuple-element.21, f32[6144,192,4]{0,1,2:T(8,128)} %get-tuple-element.20, f32[4,192]{1,0:T(4,128)S(1)} %get-tuple-element.18, f32[4,192]{1,0:T(4,128)S(1)} %get-tuple-element.17, pred[192,6144]{1,0:T(8,128)(4,1)S(1)} %fusion.25), kind=kLoop, calls=%fused_computation.15 | loop fusion | flops 33030144 | bytes 48371712 | tf_op jit(solution)/shard_map/reshape.24
  206.4 0.0 copy-start.1
  206.4 3.6 copy-done.1
  210.0 3.9 %fusion.24 = bf16[6144,1,128]{2,0,1:T(8,128)(2,1)} fusion(bf16[4,192,6144]{2,1,0:T(8,128)(2,1)S(1)} %fusion.10, bf16[192,512]{1,0:T(8,128)(2,1)S(1)} %copy-done), kind=kOutput, calls=%fused_computation.23 | convolution fusion | flops 1208745984 | bytes 11206656 | tf_op jit(solution)/shard_map/ghsk,sghd->kgd/dot_general | solution.py:85
  213.9 0.0 reduce-scatter.5.cloned.1.call-update
  213.9 6.4 %fusion.35 = bf16[192,1,4,128]{3,0,2,1:T(8,128)(2,1)S(1)} fusion(bf16[4,192,6144]{2,1,0:T(8,128)(2,1)} %copy-done.1, bf16[6144,128]{1,0:T(8,128)(2,1)S(1)} %copy-done.2), kind=kOutput, calls=%fused_computation.34 | convolution fusion | flops 1208057856 | bytes 11206656 | tf_op jit(solution)/shard_map/ghsk,kgd->sghd/dot_general | solution.py:84
  220.3 0.2 copy.28
  220.5 0.7 copy.60
  221.2 58.7 %reduce-scatter.7.cloned.1.call-done = bf16[192,128]{1,0:T(8,128)(2,1)} async-done(((bf16[6144,128]{1,0:T(8,128)(2,1)}), bf16[192,128]{1,0:T(8,128)(2,1)}) %reduce-scatter.7.cloned.1.call-update) | async-done | bytes 49168
  279.9 92.1 %reduce-scatter.5.cloned.1.call-done = bf16[192,1,128]{2,0,1:T(8,128)(2,1)} async-done(((bf16[6144,1,128]{2,0,1:T(8,128)(2,1)}), bf16[192,1,128]{2,0,1:T(8,128)(2,1)}) %reduce-scatter.5.cloned.1.call-update) | async-done | bytes 49168 | tf_op jit(solution)/shard_map/reduce_scatter | solution.py:95
  (5 shorter events, 0.0 us)
Async XLA Ops:
  7.2 106.2 %copy-start = (bf16[192,512]{1,0:T(8,128)(2,1)S(1)}, bf16[192,512]{1,0:T(8,128)(2,1)}, u32[]{:S(2)}) copy-start(bf16[192,512]{1,0:T(8,128)(2,1)} %param.6) | copy-start | bytes 589828
  7.2 49.8 %all-gather.6.cloned.1.call-start = ((), (), s32[]{:S(2)}) async-start(), calls=%async_computation.3 | async-start | bytes 1769472 | tf_op jit(solution)/shard_map/all_gather | solution.py:44
  7.9 105.4 %all-gather.4.cloned.1.call-start = ((), (), s32[]{:S(2)}) async-start(), calls=%async_computation.2 | async-start | bytes 1622016 | tf_op jit(solution)/shard_map/all_gather | solution.py:74
  8.7 157.5 %all-gather.8.cloned.1.call-start = ((), (), s32[]{:S(2)}) async-start(), calls=%async_computation.4 | async-start | bytes 1622016 | tf_op jit(solution)/shard_map/all_gather | solution.py:75
  9.4 270.5 %reduce-scatter.7.cloned.1.call-start = ((), (), s32[]{:S(2)}) async-start(), calls=%async_computation.6 | async-start | bytes 1622016
  192.5 179.5 %reduce-scatter.5.cloned.1.call-start = ((), (), s32[]{:S(2)}) async-start(), calls=%async_computation.5 | async-start | bytes 1622016 | tf_op jit(solution)/shard_map/reduce_scatter | solution.py:95
  206.4 3.6 copy-start.1
  210.0 3.9 %copy-start.2 = (bf16[6144,128]{1,0:T(8,128)(2,1)S(1)}, bf16[6144,128]{1,0:T(8,128)(2,1)}, u32[]{:S(2)}) copy-start(bf16[6144,128]{1,0:T(8,128)(2,1)} %all-gather.4.cloned.1.call-done) | copy-start | bytes 4718596
Sparse Core Ops, SparseCore 0:
  9.8 47.1 all-gather.5
  59.5 53.7 all-gather.3
  115.9 50.2 all-gather.7
  192.6 87.3 reduce-scatter.6
  284.2 87.7 reduce-scatter.4
where the time goes:
time: 379 us
  waiting for transfers between devices  293 us (77%)
  matrix products  49 us (13%)
  other arithmetic  16.2 us (4%)
  between operations  13.9 us (4%)
  local copies, waits for them, and re-layouts  6.1 us (2%)
    reduce_scatter x1, waiting for transfers between devices, shards(): lax.psum_scatter(key_terms.astype(jnp.bfloat16), 'seq', scatter_dimension...  92.1 us
    unnamed x6, waiting for transfers between devices  60.8 us
    all_gather x1, waiting for transfers between devices, shards(): key_block = lax.all_gather(keys, 'seq', axis=0, tiled=True)  52.1 us
    all_gather x1, waiting for transfers between devices, shards(): lax.all_gather(d_out, 'head', axis=1, tiled=True)  45 us
    all_gather x1, waiting for transfers between devices, shards(): value_block = lax.all_gather(values, 'seq', axis=0, tiled=True)  43 us
    dot_general x1, matrix products, softmax_grads(): jnp.einsum('sghd,kgd->ghsk', g_four, value_three, preferred_element_type=...  15.5 us
    another operation x1, other arithmetic  13.7 us
    dot_general x1, matrix products, softmax_grads(): jnp.einsum('sghd,kgd->ghsk', q_four, key_three, preferred_element_type=jn...  9.9 us
  transfers between devices with their start and end apart: 5, of which 5 were waited for; matrix products, arithmetic and copies ran while one was open for 11% of the time, Pallas kernels for 0%

commit v1 on v0

--- a/solution.py
+++ b/solution.py
@@ -71,8 +71,11 @@
     accum_new = jnp.sum(weights * grad_dots, axis=-1)
     log_total = high_new + jnp.log(total_new)
     row_delta = accum_new / total_new
-    key_block = lax.all_gather(keys, "seq", axis=0, tiled=True)
-    value_block = lax.all_gather(values, "seq", axis=0, tiled=True)
+    key_block, value_block = jnp.split(
+        lax.all_gather(jnp.concatenate([keys, values], 1), "seq", axis=0, tiled=True),
+        [keys.shape[1]],
+        1,
+    )
     piece_rows = key_block.shape[0]
     allowed = allowed_pairs(doc_starts, my_rows, jnp.arange(piece_rows, dtype=jnp.int32))
     key_three = key_block.reshape(piece_rows, groups, head_size)

time: 379 us -> 433 us (1.14)
  waiting for transfers between devices: 293 us -> 332 us
  matrix products: 49 us -> 62.2 us
  local copies, waits for them, and re-layouts: 6.1 us -> 13.5 us
  other arithmetic: 16.2 us -> 10.5 us
    all_gather x0 -> x1, waiting for transfers between devices: none -> 45.6 us  [shards(): lax.all_gather(jnp.concatenate([keys, values], 1), 'seq', axis=0, tiled=T...]
    dot_general x0 -> x2, matrix products: none -> 16.7 us  [the longest x1 11.4 us: shards(): jnp.einsum('sghd,kgd->ghsk', grad_four, value_three, preferred_element_ty...]
    another operation x1 -> x0, other arithmetic: 13.7 us -> none
    all_gather x1, waiting for transfers between devices: 43 us -> 34.7 us  [shards(): value_block = lax.all_gather(values, 'seq', axis=0, tiled=True)]
    unnamed x8, local copies, waits for them, and re-layouts: 5.95 us -> 13.4 us
    reduce_sum x0 -> x1, other arithmetic: none -> 6.46 us  [shards(): total_new = jnp.sum(weights, axis=-1)]
    dot_general x1, matrix products: 15.5 us -> 11 us  [softmax_grads(): jnp.einsum('sghd,kgd->ghsk', g_four, value_three, preferred_element_type=...]
    unnamed x6 -> x7, waiting for transfers between devices: 60.8 us -> 63.9 us
  transfers between devices with their start and end apart: 5 -> 6, of which waited for: 5 -> 6; matrix products, arithmetic and copies ran while one was open for 11% -> 12% of each run, Pallas kernels for 0% -> 0%
where the time goes in v1:
time: 433 us; the launch traced here: 432 us
  waiting for transfers between devices  332 us (77%)
  matrix products  62.2 us (14%)
  between operations  14.2 us (3%)
  local copies, waits for them, and re-layouts  13.5 us (3%)
  other arithmetic  10.5 us (2%)
    reduce_scatter x1, waiting for transfers between devices, shards(): lax.psum_scatter(key_terms.astype(jnp.bfloat16), 'seq', scatter_dimension...  92 us
    unnamed x7, waiting for transfers between devices  63.9 us
    all_gather x1, waiting for transfers between devices, shards(): key_block = lax.all_gather(keys, 'seq', axis=0, tiled=True)  52.1 us
    all_gather x1, waiting for transfers between devices, shards(): lax.all_gather(jnp.concatenate([keys, values], 1), 'seq', axis=0, tiled=T...  45.6 us
    all_gather x1, waiting for transfers between devices, shards(): lax.all_gather(d_out, 'head', axis=1, tiled=True)  43.4 us
    all_gather x1, waiting for transfers between devices, shards(): value_block = lax.all_gather(values, 'seq', axis=0, tiled=True)  34.7 us
    unnamed x8, local copies, waits for them, and re-layouts  13.4 us
    dot_general x1, matrix products, shards(): jnp.einsum('sghd,kgd->ghsk', grad_four, value_three, preferred_element_ty...  11.4 us
  transfers between devices with their start and end apart: 6, of which 6 were waited for; matrix products, arithmetic and copies ran while one was open for 12% of the time, Pallas kernels for 0%

profile of v1, /device:TPU:8, one launch (start us, length us, event | category | flops | bytes accessed | tf_op | source)
XLA Modules:
  0.0 432.5 jit_solution(7986096271883160714)
XLA Ops:
  7.2 0.7 all-gather.9.cloned.1.call-update
  7.9 0.0 all-gather.7.cloned.1.call-start
  8.0 0.7 all-gather.7.cloned.1.call-update
  8.7 0.0 all-gather.11.cloned.1.call-start
  8.7 0.7 all-gather.11.cloned.1.call-update
  9.4 0.0 all-gather.5.cloned.1.call-start
  9.4 1.5 pad_maximum_fusion
  10.9 0.0 reduce-scatter.7.cloned.1.call-start
  11.0 0.8 convert_reduce_fusion
  11.8 0.7 convert_reduce_fusion.1
  12.5 1.0 fusion.35
  13.6 43.4 %all-gather.9.cloned.1.call-done = bf16[192,4096]{1,0:T(8,128)(2,1)} async-done(((bf16[192,512]{1,0:T(8,128)(2,1)}), bf16[192,4096]{1,0:T(8,128)(2,1)}) %all-gather.9.cloned.1.call-update) | async-done | bytes 1572880 | tf_op jit(solution)/shard_map/all_gather | solution.py:44
  57.0 4.2 fusion.46
  61.2 52.1 %all-gather.7.cloned.1.call-done = bf16[6144,128]{1,0:T(8,128)(2,1)} async-done(((bf16[192,128]{1,0:T(8,128)(2,1)}), bf16[6144,128]{1,0:T(8,128)(2,1)}) %all-gather.7.cloned.1.call-update) | async-done | bytes 1572880 | tf_op jit(solution)/shard_map/all_gather | solution.py:53
  113.3 5.3 %fusion.6 = (f32[4,192]{1,0:T(4,128)S(1)}, f32[6144,192,4]{0,1,2:T(8,128)S(1)}) fusion(pred[192,6144]{1,0:T(8,128)(4,1)S(1)} %fusion.35, bf16[6144,128]{1,0:T(8,128)(2,1)} %all-gather.7.cloned.1.call-done, bf16[192,512]{1,0:T(8,128)(2,1)S(1)} %copy-done), kind=kOutput, calls=%fused_computation.11 | convolution fusion | flops 1222114560 | bytes 21826560 | tf_op jit(solution)/shard_map/sghd,kgd->ghsk/dot_general | solution.py:60
  118.6 6.4 %copy-done.1 = f32[6144,192,4]{0,1,2:T(8,128)} copy-done((f32[6144,192,4]{0,1,2:T(8,128)}, f32[6144,192,4]{0,1,2:T(8,128)S(1)}, u32[]{:S(2)}) %copy-start.1) | copy-done | bytes 18874392
  125.1 6.5 %fusion.8 = f32[4,192]{1,0:T(4,128)S(1)} fusion(f32[6144,192,4]{0,1,2:T(8,128)S(1)} %get-tuple-element.18, f32[4,192]{1,0:T(4,128)S(1)} %broadcast_maximum_fusion, pred[192,6144]{1,0:T(8,128)(4,1)S(1)} %fusion.35), kind=kLoop, calls=%fused_computation.13 | loop fusion | flops 23592192 | bytes 20060160 | tf_op jit(solution)/shard_map/reduce_sum | solution.py:70
  131.5 34.7 %all-gather.11.cloned.1.call-done = bf16[6144,128]{1,0:T(8,128)(2,1)} async-done(((bf16[192,128]{1,0:T(8,128)(2,1)}), bf16[6144,128]{1,0:T(8,128)(2,1)}) %all-gather.11.cloned.1.call-update) | async-done | bytes 1572880 | tf_op jit(solution)/shard_map/all_gather | solution.py:54
  166.2 11.4 %fusion = f32[4,192]{1,0:T(4,128)S(1)} fusion(f32[6144,192,4]{0,1,2:T(8,128)} %copy-done.1, f32[4,192]{1,0:T(4,128)S(1)} %broadcast_maximum_fusion, pred[192,6144]{1,0:T(8,128)(4,1)S(1)} %fusion.35, bf16[6144,128]{1,0:T(8,128)(2,1)} %all-gather.11.cloned.1.call-done, bf16[24,4,8,128]{3,2,1,0:T(8,128)(2,1)S(1)} %fusion.46), kind=kOutput, calls=%fused_computation.1 | convolution fusion | flops 1236270336 | bytes 21829632 | tf_op jit(solution)/shard_map/sghd,kgd->ghsk/dot_general | solution.py:67
  177.7 45.6 %all-gather.5.cloned.1.call-done = bf16[6144,256]{1,0:T(8,128)(2,1)} async-done(((bf16[192,256]{1,0:T(8,128)(2,1)}), bf16[6144,256]{1,0:T(8,128)(2,1)}) %all-gather.5.cloned.1.call-update) | async-done | bytes 3145744 | tf_op jit(solution)/shard_map/all_gather | solution.py:75
  223.3 9.3 %fusion.39 = f32[6144,192,4]{0,1,2:T(8,128)} fusion(bf16[6144,256]{1,0:T(8,128)(2,1)} %all-gather.5.cloned.1.call-done, bf16[192,512]{1,0:T(8,128)(2,1)S(1)} %copy-done), kind=kOutput, calls=%fused_computation.34 | convolution fusion | flops 1207959552 | bytes 20643840 | tf_op jit(solution)/shard_map/sghd,kgd->ghsk/dot_general | solution.py:23
  232.6 10.2 %fusion.29 = bf16[6144,128]{0,1:T(8,128)(2,1)} fusion(f32[6144,192,4]{0,1,2:T(8,128)} %fusion.39, f32[4,192]{1,0:T(4,128)S(1)} %get-tuple-element.15, pred[192,6144]{1,0:T(8,128)(4,1)S(1)} %fusion.35, bf16[24,4,8,128]{3,2,1,0:T(8,128)(2,1)S(1)} %fusion.46), kind=kOutput, calls=%fused_computation.25 | convolution fusion | flops 1227620352 | bytes 21826560 | tf_op jit(solution)/shard_map/ghsk,sghd->kgd/dot_general | solution.py:91
  242.8 2.6 copy.42
  245.5 0.0 reduce-scatter.5.cloned.1.call-start
  245.5 11.0 %fusion.3 = bf16[1,4,192,6144]{3,2,1,0:T(8,128)(2,1)S(1)} fusion(f32[6144,192,4]{0,1,2:T(8,128)} %fusion.39, f32[4,192]{1,0:T(4,128)S(1)} %get-tuple-element.16, f32[4,192]{1,0:T(4,128)S(1)} %get-tuple-element.15, pred[192,6144]{1,0:T(8,128)(4,1)S(1)} %fusion.35, bf16[6144,256]{1,0:T(8,128)(2,1)} %all-gather.5.cloned.1.call-done, ...), kind=kOutput, calls=%fused_computation.5 | convolution fusion | flops 1240989696 | bytes 31266816 | tf_op jit(solution)/shard_map/sghd,kgd->ghsk/dot_general | solution.py:27
  256.5 3.6 copy-done.2
  260.2 3.9 fusion.32
  264.0 6.9 %fusion.43 = bf16[192,1,4,128]{3,0,2,1:T(8,128)(2,1)S(1)} fusion(bf16[1,4,192,6144]{3,2,1,0:T(8,128)(2,1)} %copy-done.2, bf16[6144,256]{1,0:T(8,128)(2,1)} %all-gather.5.cloned.1.call-done), kind=kOutput, calls=%fused_computation.37 | convolution fusion | flops 1208057856 | bytes 11206656 | tf_op jit(solution)/shard_map/ghsk,kgd->sghd/dot_general | solution.py:87
  271.0 0.2 copy.36
  271.1 0.7 copy.74
  271.8 61.7 %reduce-scatter.7.cloned.1.call-done = bf16[192,128]{1,0:T(8,128)(2,1)} async-done(((bf16[6144,128]{1,0:T(8,128)(2,1)}), bf16[192,128]{1,0:T(8,128)(2,1)}) %reduce-scatter.7.cloned.1.call-update) | async-done | bytes 49168
  333.6 92.0 %reduce-scatter.5.cloned.1.call-done = bf16[192,1,128]{2,0,1:T(8,128)(2,1)} async-done(((bf16[6144,1,128]{2,0,1:T(8,128)(2,1)}), bf16[192,1,128]{2,0,1:T(8,128)(2,1)}) %reduce-scatter.5.cloned.1.call-update) | async-done | bytes 49168 | tf_op jit(solution)/shard_map/reduce_scatter | solution.py:98
  (11 shorter events, 0.1 us)
Async XLA Ops:
  7.2 106.2 %copy-start = (bf16[192,512]{1,0:T(8,128)(2,1)S(1)}, bf16[192,512]{1,0:T(8,128)(2,1)}, u32[]{:S(2)}) copy-start(bf16[192,512]{1,0:T(8,128)(2,1)} %param.6) | copy-start | bytes 589828
  7.2 49.8 %all-gather.9.cloned.1.call-start = ((), (), s32[]{:S(2)}) async-start(), calls=%async_computation.4 | async-start | bytes 1769472 | tf_op jit(solution)/shard_map/all_gather | solution.py:44
  7.9 105.4 %all-gather.7.cloned.1.call-start = ((), (), s32[]{:S(2)}) async-start(), calls=%async_computation.3 | async-start | bytes 1622016 | tf_op jit(solution)/shard_map/all_gather | solution.py:53
  8.7 157.5 %all-gather.11.cloned.1.call-start = ((), (), s32[]{:S(2)}) async-start(), calls=%async_computation.5 | async-start | bytes 1622016 | tf_op jit(solution)/shard_map/all_gather | solution.py:54
  9.4 213.9 %all-gather.5.cloned.1.call-start = ((), (), s32[]{:S(2)}) async-start(), calls=%async_computation.2 | async-start | bytes 3244032 | tf_op jit(solution)/shard_map/all_gather | solution.py:75
  10.9 322.6 %reduce-scatter.7.cloned.1.call-start = ((), (), s32[]{:S(2)}) async-start(), calls=%async_computation.7 | async-start | bytes 1622016
  118.6 6.5 %copy-start.1 = (f32[6144,192,4]{0,1,2:T(8,128)}, f32[6144,192,4]{0,1,2:T(8,128)S(1)}, u32[]{:S(2)}) copy-start(f32[6144,192,4]{0,1,2:T(8,128)S(1)} %get-tuple-element.18) | copy-start | bytes 56623108
  245.5 180.1 %reduce-scatter.5.cloned.1.call-start = ((), (), s32[]{:S(2)}) async-start(), calls=%async_computation.6 | async-start | bytes 1622016 | tf_op jit(solution)/shard_map/reduce_scatter | solution.py:98
  256.5 3.6 copy-start.2
Sparse Core Ops, SparseCore 0:
  9.8 47.1 all-gather.8
  59.5 53.7 all-gather.6
  115.9 50.2 all-gather.10
  169.2 54.0 all-gather.4
  245.6 87.9 reduce-scatter.6
  337.8 87.7 reduce-scatter.4
